TPU v7x, 32 devices: a whole 2x2x4 slice. The times are simulated.
32 devices in a mesh: wa: 2 (over x), ha: 16 (over z, y, core).
Axes of the slice: x: 2, y: 2, z: 4, core: 2. Of those that a mesh axis runs over, the one named last changes fastest.
Arguments:
- tokens: float32 [128, 5376], P('ha', 'wa'), may hold values from -6 to 6
- grad_out: float32 [128, 5376], P('ha', 'wa'), may hold values from -1.5 to 1.5
- gate_weight: float32 [5376, 10752], P('wa', 'ha'), may hold values from -0.078125 to 0.078125
- up_weight: float32 [5376, 10752], P('wa', 'ha'), may hold values from -0.078125 to 0.078125
- down_weight: float32 [10752, 5376], P('ha', 'wa'), may hold values from -0.0625 to 0.0625
Outputs:
- grad_tokens: float32 [128, 5376], P('ha', 'wa')
- grad_gate: float32 [5376, 10752], P('wa', 'ha')
- grad_up: float32 [5376, 10752], P('wa', 'ha')
- grad_down: float32 [10752, 5376], P('ha', 'wa')
All inputs are finite; a program needn't handle non-finite values.
Results may differ from a plain program's by a relative error of at most 0.00018.
Values sent between devices are 32-bit elements; how exact they have to be, the bound alone decides.
No kernel may reach another device: no remote copies, remote signals or barrier semaphores. Data moves between devices by JAX's collectives and lax.ppermute only.
A program may use at most 128 MiB of HBM per device.

v0:
```python
import jax
import jax.numpy as jnp
from jax import lax
from jax.sharding import PartitionSpec as P


def contract(left, right, left_dim, right_dim):
    return lax.dot_general(
        left,
        right,
        (((left_dim,), (right_dim,)), ((), ())),
        preferred_element_type=jnp.float32,
        precision=lax.Precision.HIGHEST,
    )


def derivs(gate, up, grad_hidden):
    sig = 1.0 / (1.0 + jnp.exp(-gate))
    hidden = gate * sig * up
    grad_up_act = grad_hidden * gate * sig
    grad_gate_act = grad_hidden * up * sig * (1.0 + gate * (1.0 - sig))
    return (hidden, grad_gate_act, grad_up_act)


def per_device(tokens, grad_out, gate_weight, up_weight, down_weight):
    inputs, upstream = (
        lax.all_gather(tokens, "ha", axis=0, tiled=True),
        lax.all_gather(grad_out, "ha", axis=0, tiled=True),
    )
    width = gate_weight.shape[1]
    gate = contract(inputs, gate_weight, 1, 0)
    up = contract(inputs, up_weight, 1, 0)
    grad_hidden = contract(upstream, down_weight, 1, 1)
    summed = lax.psum(jnp.concatenate([gate, up, grad_hidden], axis=1), "wa")
    hidden, grad_gate_act, grad_up_act = derivs(
        summed[:, :width], summed[:, width : 2 * width], summed[:, 2 * width :]
    )
    grad_down = contract(hidden, upstream, 0, 0)
    grad_gate = contract(inputs, grad_gate_act, 0, 0)
    grad_up = contract(inputs, grad_up_act, 0, 0)
    grad_tokens = lax.psum_scatter(
        contract(grad_gate_act, gate_weight, 1, 1) + contract(grad_up_act, up_weight, 1, 1),
        "ha",
        scatter_dimension=0,
        tiled=True,
    )
    return (grad_tokens, grad_gate, grad_up, grad_down)


def solution(mesh):
    placed = (P("ha", "wa"), P("ha", "wa"), P("wa", "ha"), P("wa", "ha"), P("ha", "wa"))
    return jax.shard_map(
        per_device,
        mesh=mesh,
        in_specs=placed,
        out_specs=(P("ha", "wa"), P("wa", "ha"), P("wa", "ha"), P("ha", "wa")),
        check_vma=False,
    )
```

profile of v0, /device:TPU:0, one launch (start us, length us, event | category | flops | bytes accessed | tf_op | source)
XLA Modules:
  0.0 260.4 jit_solution(12057325725351221263)
XLA Ops:
  7.2 0.0 all-gather.3.cloned.1.call-start
  7.2 0.7 all-gather.3.cloned.1.call-update
  7.9 0.0 all-gather.5.cloned.1.call-start
  7.9 0.7 all-gather.5.cloned.1.call-update
  8.6 0.0 all-reduce.4.cloned.1.call-start
  8.7 43.1 %all-gather.3.cloned.1.call-done = f32[128,2688]{1,0:T(8,128)} async-done(((f32[8,2688]{1,0:T(8,128)}), f32[128,2688]{1,0:T(8,128)}) %all-gather.3.cloned.1.call-update) | async-done | bytes 1376272 | tf_op jit(solution)/shard_map/all_gather | solution.py:27
  51.8 0.0 copy-start
  51.8 0.0 copy-start.1
  51.8 8.8 %fusion.9 = f32[128,672]{0,1:T(8,128)S(1)} fusion(f32[128,2688]{1,0:T(8,128)} %all-gather.3.cloned.1.call-done, f32[2688,672]{0,1:T(8,128)} %param.8), kind=kOutput, calls=%fused_computation.17 | convolution fusion | flops 2774532096 | bytes 8945664 | tf_op jit(solution)/shard_map/dot_general | solution.py:8
  60.7 0.0 copy-done
  60.7 0.0 copy-done.1
  60.7 6.1 %fusion.8 = f32[128,672]{0,1:T(8,128)S(1)} fusion(f32[128,2688]{1,0:T(8,128)S(1)} %copy-done.1, f32[2688,672]{0,1:T(8,128)S(1)} %copy-done), kind=kOutput, calls=%fused_computation.16 | convolution fusion | flops 2774532096 | bytes 8945664 | tf_op jit(solution)/shard_map/dot_general | solution.py:8
  66.8 25.1 %all-gather.5.cloned.1.call-done = f32[128,2688]{1,0:T(8,128)} async-done(((f32[8,2688]{1,0:T(8,128)}), f32[128,2688]{1,0:T(8,128)}) %all-gather.5.cloned.1.call-update) | async-done | bytes 1376272 | tf_op jit(solution)/shard_map/all_gather | solution.py:28
  91.8 8.7 %fusion.10 = f32[128,672]{0,1:T(8,128)S(1)} fusion(f32[128,2688]{1,0:T(8,128)} %all-gather.5.cloned.1.call-done, f32[672,2688]{1,0:T(8,128)} %param.9), kind=kOutput, calls=%fused_computation.18 | convolution fusion | flops 2774532096 | bytes 8945664 | tf_op jit(solution)/shard_map/dot_general | solution.py:8
  100.5 0.0 copy-start.3
  100.5 1.0 pad_maximum_fusion
  101.6 0.0 all-reduce.4.cloned.1.call-update
  101.6 0.0 all-reduce.6.cloned.1.call-start
  101.6 0.0 copy-done.3
  101.7 0.6 dynamic-slice
  102.9 37.5 %all-reduce.4.cloned.1.call-done = f32[128,2016]{0,1:T(8,128)} async-done(((f32[128,2016]{0,1:T(8,128)}), f32[128,2016]{0,1:T(8,128)}) %all-reduce.4.cloned.1.call-update) | async-done | bytes 1032208 | tf_op jit(solution)/shard_map/psum | solution.py:34
  140.3 0.0 copy-start.2
  140.3 8.3 %fusion.7 = f32[128,2688]{1,0:T(8,128)S(1)} fusion(f32[2688,672]{0,1:T(8,128)} %param.7, f32[128,2016]{0,1:T(8,128)} %all-reduce.4.cloned.1.call-done), kind=kOutput, calls=%fused_computation.15 | convolution fusion | flops 2775306240 | bytes 9633792 | tf_op jit(solution)/shard_map/dot_general | solution.py:8
  148.6 0.0 copy-done.2
  148.6 8.4 %convolution_add_fusion = f32[128,2688]{1,0:T(8,128)} fusion(f32[128,2688]{1,0:T(8,128)S(1)} %fusion.7, f32[2688,672]{0,1:T(8,128)} %param.8, f32[128,2016]{0,1:T(8,128)S(1)} %copy-done.2), kind=kOutput, calls=%fused_computation.2 | convolution fusion | flops 2775306240 | bytes 10665984 | tf_op jit(solution)/shard_map/dot_general | solution.py:8
  157.0 0.0 all-reduce.6.cloned.1.call-update
  157.1 9.2 %fusion = f32[672,2688]{1,0:T(8,128)} fusion(f32[128,2688]{1,0:T(8,128)} %all-gather.5.cloned.1.call-done, f32[128,2016]{0,1:T(8,128)S(1)} %copy-done.2), kind=kOutput, calls=%fused_computation.4 | convolution fusion | flops 2774962176 | bytes 9289728 | tf_op jit(solution)/shard_map/dot_general | solution.py:8
  166.2 7.9 %convolution_bitcast_fusion.1 = f32[2688,672]{0,1:T(8,128)} fusion(f32[128,2688]{1,0:T(8,128)S(1)} %copy-done.1, f32[128,2016]{0,1:T(8,128)S(1)} %copy-done.2), kind=kOutput, calls=%fused_computation.1 | convolution fusion | flops 2775306240 | bytes 9633792 | tf_op jit(solution)/shard_map/dot_general | solution.py:8
  174.1 7.8 %convolution_bitcast_fusion = f32[2688,672]{0,1:T(8,128)} fusion(f32[128,2688]{1,0:T(8,128)S(1)} %copy-done.1, f32[128,2016]{0,1:T(8,128)S(1)} %copy-done.2), kind=kOutput, calls=%fused_computation | convolution fusion | flops 2774962176 | bytes 9289728 | tf_op jit(solution)/shard_map/dot_general | solution.py:8
  181.9 70.4 %all-reduce.6.cloned.1.call-done = f32[128,2688]{1,0:T(8,128)} async-done(((f32[128,2688]{1,0:T(8,128)}), f32[128,2688]{1,0:T(8,128)}) %all-reduce.6.cloned.1.call-update) | async-done | bytes 1376272
  252.3 1.5 constant_dynamic-slice_fusion
Async XLA Ops:
  7.2 44.7 %all-gather.3.cloned.1.call-start = ((), (), s32[]{:S(2)}) async-start(), calls=%async_computation | async-start | bytes 1462272 | tf_op jit(solution)/shard_map/all_gather | solution.py:27
  7.9 83.9 %all-gather.5.cloned.1.call-start = ((), (), s32[]{:S(2)}) async-start(), calls=%async_computation.1 | async-start | bytes 1462272 | tf_op jit(solution)/shard_map/all_gather | solution.py:28
  8.6 131.7 %all-reduce.4.cloned.1.call-start = ((), (), s32[]{:S(2)}) async-start(), calls=%async_computation.2 | async-start | bytes 2064384 | tf_op jit(solution)/shard_map/psum | solution.py:34
  51.8 8.8 %copy-start = (f32[2688,672]{0,1:T(8,128)S(1)}, f32[2688,672]{0,1:T(8,128)}, u32[]{:S(2)}) copy-start(f32[2688,672]{0,1:T(8,128)} %param.7) | copy-start | bytes 21676036
  51.8 8.8 %copy-start.1 = (f32[128,2688]{1,0:T(8,128)S(1)}, f32[128,2688]{1,0:T(8,128)}, u32[]{:S(2)}) copy-start(f32[128,2688]{1,0:T(8,128)} %all-gather.3.cloned.1.call-done) | copy-start | bytes 4128772
  100.5 1.1 copy-start.3
  101.6 150.7 %all-reduce.6.cloned.1.call-start = ((), (), s32[]{:S(2)}) async-start(), calls=%async_computation.3 | async-start | bytes 2752512
  140.3 8.3 %copy-start.2 = (f32[128,2016]{0,1:T(8,128)S(1)}, f32[128,2016]{0,1:T(8,128)}, u32[]{:S(2)}) copy-start(f32[128,2016]{0,1:T(8,128)} %all-reduce.4.cloned.1.call-done) | copy-start | bytes 3096580
Sparse Core Ops, SparseCore 0:
  10.1 41.6 all-gather.2
  54.0 37.7 all-gather.4
  101.7 38.5 all-reduce.3
  157.2 95.1 all-reduce.5
where the time goes:
time: 261 us; the launch traced here: 260 us
  waiting for transfers between devices  178 us (68%)
  matrix products  65 us (25%)
  between operations  14.5 us (6%)
    unnamed x5, waiting for transfers between devices  71.9 us
    dot_general x8, matrix products, contract(): lax.dot_general(left, right, (((left_dim,), (right_dim,)), ((), ())), pre...  65 us
    all_gather x1, waiting for transfers between devices, per_device(): lax.all_gather(tokens, 'ha', axis=0, tiled=True)  43.1 us
    psum x1, waiting for transfers between devices, per_device(): summed = lax.psum(jnp.concatenate([gate, up, grad_hidden], axis=1), 'wa')  37.5 us
    all_gather x1, waiting for transfers between devices, per_device(): lax.all_gather(grad_out, 'ha', axis=0, tiled=True)  25.1 us
  transfers between devices with their start and end apart: 4, of which 4 were waited for; matrix products, arithmetic and copies ran while one was open for 15% of the time, Pallas kernels for 0%

commit v1 on v0

v1 whole, which is shorter than its diff:
```python
import jax
import jax.numpy as jnp
from jax import lax
from jax.sharding import PartitionSpec as P


def contract(left, right, left_dim, right_dim):
    return lax.dot_general(
        left,
        right,
        (((left_dim,), (right_dim,)), ((), ())),
        preferred_element_type=jnp.float32,
        precision=lax.Precision.HIGH,
    )


def derivs(gate, up, grad_hidden):
    sig = 1.0 / (1.0 + jnp.exp(-gate))
    hidden = gate * sig * up
    grad_up_act = grad_hidden * gate * sig
    grad_gate_act = grad_hidden * up * sig * (1.0 + gate * (1.0 - sig))
    return (hidden, grad_gate_act, grad_up_act)


def swap(x, axis, size, bit):
    return lax.ppermute(x, axis, [(i, i ^ bit) for i in range(size)])


def bits_of(size):
    assert size & (size - 1) == 0
    return [1 << b for b in reversed(range(size.bit_length() - 1))]


def gather(x, axis, size):
    for bit in bits_of(size):
        x = jnp.concatenate([x, swap(x, axis, size, bit)], axis=0)
    return x


def scatter_sum(x, axis, size):
    for bit in reversed(bits_of(size)):
        half = x.shape[0] // 2
        x = x[:half] + swap(x[half:], axis, size, bit)
    return x


def all_sum(x, axis, size):
    for bit in bits_of(size):
        x = x + swap(x, axis, size, bit)
    return x


def solution(mesh):
    nw, nh = mesh.shape["wa"], mesh.shape["ha"]

    def per_device(tokens, grad_out, gate_weight, up_weight, down_weight):
        inputs = gather(tokens, "ha", nh)
        upstream = gather(grad_out, "ha", nh)
        gate = all_sum(contract(inputs, gate_weight, 1, 0), "wa", nw)
        up = all_sum(contract(inputs, up_weight, 1, 0), "wa", nw)
        grad_hidden = all_sum(contract(upstream, down_weight, 1, 1), "wa", nw)
        hidden, grad_gate_act, grad_up_act = derivs(gate, up, grad_hidden)
        grad_tokens = scatter_sum(
            contract(grad_gate_act, gate_weight, 1, 1) + contract(grad_up_act, up_weight, 1, 1),
            "ha",
            nh,
        )
        grad_down = contract(hidden, upstream, 0, 0)
        grad_gate = contract(inputs, grad_gate_act, 0, 0)
        grad_up = contract(inputs, grad_up_act, 0, 0)
        return (grad_tokens, grad_gate, grad_up, grad_down)

    placed = (P("ha", "wa"), P("ha", "wa"), P("wa", "ha"), P("wa", "ha"), P("ha", "wa"))
    return jax.shard_map(
        per_device,
        mesh=mesh,
        in_specs=placed,
        out_specs=(P("ha", "wa"), P("wa", "ha"), P("wa", "ha"), P("ha", "wa")),
        check_vma=False,
    )
```

time: 261 us -> 96.5 us (0.37)
  waiting for transfers between devices: 178 us -> 41.6 us
  matrix products: 65 us -> 28.9 us
  starting transfers between devices: 0.16 us -> 19.9 us
  between operations: 14.5 us -> 0.86 us
    unnamed x5 -> x0, waiting for transfers between devices: 71.9 us -> none
    all_gather x2 -> x0, waiting for transfers between devices: 68.2 us -> none  [the longest x1 43.1 us: per_device(): lax.all_gather(tokens, 'ha', axis=0, tiled=True)]
    ppermute x0 -> x15, waiting for transfers between devices: none -> 41.6 us  [swap(): return lax.ppermute(x, axis, [(i, i ^ bit) for i in range(size)])]
    psum x1 -> x0, waiting for transfers between devices: 37.5 us -> none  [per_device(): summed = lax.psum(jnp.concatenate([gate, up, grad_hidden], axis=1), 'wa')]
    dot_general x8, matrix products: 65 us -> 28.9 us  [contract(): lax.dot_general(left, right, (((left_dim,), (right_dim,)), ((), ())), pre...]
    ppermute x0 -> x15, starting transfers between devices: none -> 19.9 us  [swap(): return lax.ppermute(x, axis, [(i, i ^ bit) for i in range(size)])]
  transfers between devices with their start and end apart: 4 -> 15, of which waited for: 4 -> 10; matrix products, arithmetic and copies ran while one was open for 15% -> 29% of each run, Pallas kernels for 0% -> 0%
where the time goes in v1:
time: 96.5 us; the launch traced here: 96.3 us
  waiting for transfers between devices  41.6 us (43%)
  matrix products  28.9 us (30%)
  starting transfers between devices  19.9 us (21%)
  other arithmetic  2.92 us (3%)
  local copies, waits for them, and re-layouts  2.09 us (2%)
    ppermute x15, waiting for transfers between devices, swap(): return lax.ppermute(x, axis, [(i, i ^ bit) for i in range(size)])  41.6 us
    dot_general x8, matrix products, contract(): lax.dot_general(left, right, (((left_dim,), (right_dim,)), ((), ())), pre...  28.9 us
    ppermute x15, starting transfers between devices, swap(): return lax.ppermute(x, axis, [(i, i ^ bit) for i in range(size)])  19.9 us
    concatenate x6, other arithmetic, gather(): x = jnp.concatenate([x, swap(x, axis, size, bit)], axis=0)  1.96 us
  transfers between devices with their start and end apart: 15, of which 10 were waited for; matrix products, arithmetic and copies ran while one was open for 29% of the time, Pallas kernels for 0%

profile of v1, /device:TPU:0, one launch (start us, length us, event | category | flops | bytes accessed | tf_op | source)
XLA Modules:
  0.0 96.3 jit_solution(1636314398397208671)
XLA Ops:
  0.6 0.0 copy-start.3
  0.6 0.0 copy-start.4
  0.7 4.1 %collective-permute-start.5 = (f32[8,2688]{1,0:T(8,128)}, f32[8,2688]{1,0:T(8,128)S(1)}, u32[]{:S(2)}, u32[]{:S(2)}) collective-permute-start(f32[8,2688]{1,0:T(8,128)} %param.5), channel_id=1, source_target_pairs={{0,8},{1,9},{2,10},{3,11},{4,12},{5,13},{6,14},{7,15},{8,0},{9,1},... | collective-permute-start | bytes 258056 | tf_op jit(solution)/shard_map/ppermute | solution.py:26
  4.8 0.1 collective-permute-start
  4.9 0.9 constant_dynamic-update-slice_fusion.9
  5.8 0.9 constant_dynamic-update-slice_fusion.4
  6.7 5.1 %collective-permute-done.5 = f32[8,2688]{1,0:T(8,128)S(1)} collective-permute-done((f32[8,2688]{1,0:T(8,128)}, f32[8,2688]{1,0:T(8,128)S(1)}, u32[]{:S(2)}, u32[]{:S(2)}) %collective-permute-start.5) | collective-permute-done | bytes 86048 | tf_op jit(solution)/shard_map/ppermute | solution.py:26
  11.8 0.9 pad_maximum_fusion.5
  12.7 0.4 collective-permute-start.6
  13.1 0.0 collective-permute-done
  13.1 0.9 pad_maximum_fusion.4
  14.0 1.7 %collective-permute-start.1 = (f32[16,2688]{1,0:T(8,128)S(1)}, f32[16,2688]{1,0:T(8,128)S(1)}, u32[]{:S(2)}, u32[]{:S(2)}) collective-permute-start(f32[16,2688]{1,0:T(8,128)S(1)} %pad_maximum_fusion.4), channel_id=1, source_target_pairs={{0,4},{1,5},{2,6},{3,7},{4,0},{5,1},{6,2},{7,3},{8,12},{9,13},{10,... | collective-permute-start | bytes 516104 | tf_op jit(solution)/shard_map/ppermute | solution.py:26
  15.8 4.2 %collective-permute-done.6 = f32[16,2688]{1,0:T(8,128)S(1)} collective-permute-done((f32[16,2688]{1,0:T(8,128)S(1)}, f32[16,2688]{1,0:T(8,128)S(1)}, u32[]{:S(2)}, u32[]{:S(2)}) %collective-permute-start.6) | collective-permute-done | bytes 172064 | tf_op jit(solution)/shard_map/ppermute | solution.py:26
  20.0 1.6 %collective-permute-start.7 = (f32[32,2688]{1,0:T(8,128)S(1)}, f32[32,2688]{1,0:T(8,128)S(1)}, u32[]{:S(2)}, u32[]{:S(2)}) collective-permute-start(f32[32,2688]{1,0:T(8,128)S(1)} %pad_maximum_fusion.3), channel_id=1, source_target_pairs={{0,2},{1,3},{2,0},{3,1},{4,6},{5,7},{6,4},{7,5},{8,10},{9,11},{10,... | collective-permute-start | bytes 1032200 | tf_op jit(solution)/shard_map/ppermute | solution.py:26
  21.6 0.2 collective-permute-done.1
  21.9 1.6 %collective-permute-start.2 = (f32[32,2688]{1,0:T(8,128)S(1)}, f32[32,2688]{1,0:T(8,128)S(1)}, u32[]{:S(2)}, u32[]{:S(2)}) collective-permute-start(f32[32,2688]{1,0:T(8,128)S(1)} %pad_maximum_fusion.2), channel_id=1, source_target_pairs={{0,2},{1,3},{2,0},{3,1},{4,6},{5,7},{6,4},{7,5},{8,10},{9,11},{10,... | collective-permute-start | bytes 1032200 | tf_op jit(solution)/shard_map/ppermute | solution.py:26
  23.5 6.7 %collective-permute-done.7 = f32[32,2688]{1,0:T(8,128)S(1)} collective-permute-done((f32[32,2688]{1,0:T(8,128)S(1)}, f32[32,2688]{1,0:T(8,128)S(1)}, u32[]{:S(2)}, u32[]{:S(2)}) %collective-permute-start.7) | collective-permute-done | bytes 344096 | tf_op jit(solution)/shard_map/ppermute | solution.py:26
  30.2 0.1 pad_maximum_fusion.1
  30.2 0.1 collective-permute-start.8
  30.3 3.5 %collective-permute-done.2 = f32[32,2688]{1,0:T(8,128)S(1)} collective-permute-done((f32[32,2688]{1,0:T(8,128)S(1)}, f32[32,2688]{1,0:T(8,128)S(1)}, u32[]{:S(2)}, u32[]{:S(2)}) %collective-permute-start.2) | collective-permute-done | bytes 344096 | tf_op jit(solution)/shard_map/ppermute | solution.py:26
  33.9 0.1 collective-permute-start.3
  34.1 0.0 collective-permute-done.8
  34.1 0.0 copy-start.1
  34.1 3.0 %fusion.8 = f32[128,672]{0,1:T(8,128)S(1)} fusion(f32[128,2688]{1,0:T(8,128)S(1)} %constant_dynamic-update-slice_fusion.5, f32[2688,672]{0,1:T(8,128)S(1)} %copy-done), kind=kOutput, calls=%fused_computation.32 | convolution fusion | flops 1387266048 | bytes 8945664 | tf_op jit(solution)/shard_map/dot_general | solution.py:8
  37.1 1.3 %collective-permute-start.9 = (f32[128,672]{0,1:T(8,128)S(1)}, f32[128,672]{0,1:T(8,128)S(1)}, u32[]{:S(2)}, u32[]{:S(2)}) collective-permute-start(f32[128,672]{0,1:T(8,128)S(1)} %fusion.8), channel_id=1, source_target_pairs={{0,16},{16,0},{1,17},{17,1},{2,18},{18,2},{3,19},{19,3},{4,20},{20... | collective-permute-start | bytes 1032200 | tf_op jit(solution)/shard_map/ppermute | solution.py:26
  38.4 3.0 %fusion.9 = f32[128,672]{0,1:T(8,128)S(1)} fusion(f32[128,2688]{1,0:T(8,128)S(1)} %constant_dynamic-update-slice_fusion.5, f32[2688,672]{0,1:T(8,128)S(1)} %copy-done.1), kind=kOutput, calls=%fused_computation.33 | convolution fusion | flops 1387266048 | bytes 8945664 | tf_op jit(solution)/shard_map/dot_general | solution.py:8
  41.4 0.9 collective-permute-start.10
  42.3 0.0 collective-permute-done.3
  42.3 3.0 %fusion.7 = f32[128,672]{0,1:T(8,128)S(1)} fusion(f32[128,2688]{1,0:T(8,128)S(1)} %constant_dynamic-update-slice_fusion, f32[672,2688]{1,0:T(8,128)S(1)} %copy-done.2), kind=kOutput, calls=%fused_computation.31 | convolution fusion | flops 1387266048 | bytes 8945664 | tf_op jit(solution)/shard_map/dot_general | solution.py:8
  45.3 1.3 %collective-permute-start.4 = (f32[128,672]{0,1:T(8,128)S(1)}, f32[128,672]{0,1:T(8,128)S(1)}, u32[]{:S(2)}, u32[]{:S(2)}) collective-permute-start(f32[128,672]{0,1:T(8,128)S(1)} %fusion.7), channel_id=1, source_target_pairs={{0,16},{16,0},{1,17},{17,1},{2,18},{18,2},{3,19},{19,3},{4,20},{20... | collective-permute-start | bytes 1032200 | tf_op jit(solution)/shard_map/ppermute | solution.py:26
  46.6 1.5 %collective-permute-done.9 = f32[128,672]{0,1:T(8,128)S(1)} collective-permute-done((f32[128,672]{0,1:T(8,128)S(1)}, f32[128,672]{0,1:T(8,128)S(1)}, u32[]{:S(2)}, u32[]{:S(2)}) %collective-permute-start.9) | collective-permute-done | bytes 344096 | tf_op jit(solution)/shard_map/ppermute | solution.py:26
  48.1 7.4 %collective-permute-done.10 = f32[128,672]{0,1:T(8,128)S(1)} collective-permute-done((f32[128,672]{0,1:T(8,128)S(1)}, f32[128,672]{0,1:T(8,128)S(1)}, u32[]{:S(2)}, u32[]{:S(2)}) %collective-permute-start.10) | collective-permute-done | bytes 344096 | tf_op jit(solution)/shard_map/ppermute | solution.py:26
  55.5 6.9 %collective-permute-done.4 = f32[128,672]{0,1:T(8,128)S(1)} collective-permute-done((f32[128,672]{0,1:T(8,128)S(1)}, f32[128,672]{0,1:T(8,128)S(1)}, u32[]{:S(2)}, u32[]{:S(2)}) %collective-permute-start.4) | collective-permute-done | bytes 344096 | tf_op jit(solution)/shard_map/ppermute | solution.py:26
  62.4 0.2 add_multiply_fusion
  62.6 2.6 %fusion.10 = f32[128,2688]{1,0:T(8,128)S(1)} fusion(f32[128,672]{0,1:T(8,128)S(1)} %get-tuple-element.5, f32[2688,672]{0,1:T(8,128)S(1)} %copy-done), kind=kOutput, calls=%fused_computation.34 | convolution fusion | flops 1387266048 | bytes 8945664 | tf_op jit(solution)/shard_map/dot_general | solution.py:8
  65.2 2.5 %convolution_add_fusion = f32[128,2688]{1,0:T(8,128)S(1)} fusion(f32[128,2688]{1,0:T(8,128)S(1)} %fusion.10, f32[128,672]{0,1:T(8,128)S(1)} %get-tuple-element.4, f32[2688,672]{0,1:T(8,128)S(1)} %copy-done.1), kind=kOutput, calls=%fused_computation | convolution fusion | flops 1387610112 | bytes 10321920 | tf_op jit(solution)/shard_map/dot_general | solution.py:8
  67.8 0.1 collective-permute-start.11
  67.8 2.1 %collective-permute-done.11 = f32[64,2688]{1,0:T(8,128)S(1)} collective-permute-done((f32[64,2688]{1,0:T(8,128)S(1)}, f32[64,2688]{1,0:T(8,128)S(1)}, u32[]{:S(2)}, u32[]{:S(2)}) %collective-permute-start.11) | collective-permute-done | bytes 688160 | tf_op jit(solution)/shard_map/ppermute | solution.py:26
  70.0 0.1 slice_add_fusion
  70.1 1.3 %collective-permute-start.12 = (f32[32,2688]{1,0:T(8,128)S(1)}, f32[32,2688]{1,0:T(8,128)S(1)}, u32[]{:S(2)}, u32[]{:S(2)}) collective-permute-start(f32[32,2688]{1,0:T(8,128)S(1)} %slice.35), channel_id=1, source_target_pairs={{0,2},{1,3},{2,0},{3,1},{4,6},{5,7},{6,4},{7,5},{8,10},{9,11},{10,... | collective-permute-start | bytes 1032200 | tf_op jit(solution)/shard_map/ppermute | solution.py:26
  71.4 5.0 %fusion = f32[672,2688]{1,0:T(8,128)} fusion(f32[128,2688]{1,0:T(8,128)S(1)} %constant_dynamic-update-slice_fusion, f32[128,672]{0,1:T(8,128)S(1)} %fusion.8, f32[128,672]{0,1:T(8,128)S(1)} %collective-permute-done.9, f32[128,672]{0,1:T(8,128)S(1)} %fusion.9, f32[128,672]{0,1:T(8,128)S(1)} %collective-permute-done.10), kind=kOutput, calls=%fused_computation.7 | convolution fusion | flops 1387868160 | bytes 9977856 | tf_op jit(solution)/shard_map/dot_general | solution.py:8
  76.4 3.9 %collective-permute-done.12 = f32[32,2688]{1,0:T(8,128)S(1)} collective-permute-done((f32[32,2688]{1,0:T(8,128)S(1)}, f32[32,2688]{1,0:T(8,128)S(1)}, u32[]{:S(2)}, u32[]{:S(2)}) %collective-permute-start.12) | collective-permute-done | bytes 344096 | tf_op jit(solution)/shard_map/ppermute | solution.py:26
  80.3 2.0 %collective-permute-start.13 = (f32[16,2688]{1,0:T(8,128)S(1)}, f32[16,2688]{1,0:T(8,128)S(1)}, u32[]{:S(2)}, u32[]{:S(2)}) collective-permute-start(f32[16,2688]{1,0:T(8,128)S(1)} %slice.37), channel_id=1, source_target_pairs={{0,4},{1,5},{2,6},{3,7},{4,0},{5,1},{6,2},{7,3},{8,12},{9,13},{10,... | collective-permute-start | bytes 516104 | tf_op jit(solution)/shard_map/ppermute | solution.py:26
  82.3 5.0 %fusion.11 = f32[2688,672]{0,1:T(8,128)} fusion(f32[128,2688]{1,0:T(8,128)S(1)} %constant_dynamic-update-slice_fusion.5, f32[128,672]{0,1:T(8,128)S(1)} %get-tuple-element.4), kind=kOutput, calls=%fused_computation.35 | convolution fusion | flops 1387266048 | bytes 8945664 | tf_op jit(solution)/shard_map/dot_general | solution.py:8
  87.3 3.3 %collective-permute-start.14 = (f32[8,2688]{1,0:T(8,128)S(1)}, f32[8,2688]{1,0:T(8,128)S(1)}, u32[]{:S(2)}, u32[]{:S(2)}) collective-permute-start(f32[8,2688]{1,0:T(8,128)S(1)} %slice.39), channel_id=1, source_target_pairs={{0,8},{1,9},{2,10},{3,11},{4,12},{5,13},{6,14},{7,15},{8,0},{9,1},... | collective-permute-start | bytes 258056 | tf_op jit(solution)/shard_map/ppermute | solution.py:26
  90.7 5.0 %fusion.12 = f32[2688,672]{0,1:T(8,128)} fusion(f32[128,2688]{1,0:T(8,128)S(1)} %constant_dynamic-update-slice_fusion.5, f32[128,672]{0,1:T(8,128)S(1)} %get-tuple-element.5), kind=kOutput, calls=%fused_computation.36 | convolution fusion | flops 1387266048 | bytes 8945664 | tf_op jit(solution)/shard_map/dot_general | solution.py:8
  95.6 0.0 collective-permute-done.14
  95.6 0.6 slice_add_fusion.3
  (25 shorter events, 0.5 us)
Async XLA Ops:
  0.6 19.4 %copy-start.3 = (f32[8,2688]{1,0:T(8,128)S(1)}, f32[8,2688]{1,0:T(8,128)}, u32[]{:S(2)}) copy-start(f32[8,2688]{1,0:T(8,128)} %param.5) | copy-start | bytes 258052
  0.6 21.2 %copy-start.4 = (f32[8,2688]{1,0:T(8,128)S(1)}, f32[8,2688]{1,0:T(8,128)}, u32[]{:S(2)}) copy-start(f32[8,2688]{1,0:T(8,128)} %param.6) | copy-start | bytes 258052
  0.7 11.1 %collective-permute-start.5 = (f32[8,2688]{1,0:T(8,128)}, f32[8,2688]{1,0:T(8,128)S(1)}, u32[]{:S(2)}, u32[]{:S(2)}) collective-permute-start(f32[8,2688]{1,0:T(8,128)} %param.5), channel_id=1, source_target_pairs={{0,8},{1,9},{2,10},{3,11},{4,12},{5,13},{6,14},{7,15},{8,0},{9,1},... | collective-permute-start | bytes 258056 | tf_op jit(solution)/shard_map/ppermute | solution.py:26
  4.8 8.3 %collective-permute-start = (f32[8,2688]{1,0:T(8,128)}, f32[8,2688]{1,0:T(8,128)S(1)}, u32[]{:S(2)}, u32[]{:S(2)}) collective-permute-start(f32[8,2688]{1,0:T(8,128)} %param.6), channel_id=1, source_target_pairs={{0,8},{1,9},{2,10},{3,11},{4,12},{5,13},{6,14},{7,15},{8,0},{9,1},... | collective-permute-start | bytes 258056 | tf_op jit(solution)/shard_map/ppermute | solution.py:26
  12.7 7.3 %collective-permute-start.6 = (f32[16,2688]{1,0:T(8,128)S(1)}, f32[16,2688]{1,0:T(8,128)S(1)}, u32[]{:S(2)}, u32[]{:S(2)}) collective-permute-start(f32[16,2688]{1,0:T(8,128)S(1)} %pad_maximum_fusion.5), channel_id=1, source_target_pairs={{0,4},{1,5},{2,6},{3,7},{4,0},{5,1},{6,2},{7,3},{8,12},{9,13},{10,... | collective-permute-start | bytes 516104 | tf_op jit(solution)/shard_map/ppermute | solution.py:26
  14.0 7.8 %collective-permute-start.1 = (f32[16,2688]{1,0:T(8,128)S(1)}, f32[16,2688]{1,0:T(8,128)S(1)}, u32[]{:S(2)}, u32[]{:S(2)}) collective-permute-start(f32[16,2688]{1,0:T(8,128)S(1)} %pad_maximum_fusion.4), channel_id=1, source_target_pairs={{0,4},{1,5},{2,6},{3,7},{4,0},{5,1},{6,2},{7,3},{8,12},{9,13},{10,... | collective-permute-start | bytes 516104 | tf_op jit(solution)/shard_map/ppermute | solution.py:26
  20.0 14.1 %copy-start = (f32[2688,672]{0,1:T(8,128)S(1)}, f32[2688,672]{0,1:T(8,128)}, u32[]{:S(2)}) copy-start(f32[2688,672]{0,1:T(8,128)} %param.8) | copy-start | bytes 21676036
  20.0 10.1 %collective-permute-start.7 = (f32[32,2688]{1,0:T(8,128)S(1)}, f32[32,2688]{1,0:T(8,128)S(1)}, u32[]{:S(2)}, u32[]{:S(2)}) collective-permute-start(f32[32,2688]{1,0:T(8,128)S(1)} %pad_maximum_fusion.3), channel_id=1, source_target_pairs={{0,2},{1,3},{2,0},{3,1},{4,6},{5,7},{6,4},{7,5},{8,10},{9,11},{10,... | collective-permute-start | bytes 1032200 | tf_op jit(solution)/shard_map/ppermute | solution.py:26
  21.9 12.0 %collective-permute-start.2 = (f32[32,2688]{1,0:T(8,128)S(1)}, f32[32,2688]{1,0:T(8,128)S(1)}, u32[]{:S(2)}, u32[]{:S(2)}) collective-permute-start(f32[32,2688]{1,0:T(8,128)S(1)} %pad_maximum_fusion.2), channel_id=1, source_target_pairs={{0,2},{1,3},{2,0},{3,1},{4,6},{5,7},{6,4},{7,5},{8,10},{9,11},{10,... | collective-permute-start | bytes 1032200 | tf_op jit(solution)/shard_map/ppermute | solution.py:26
  30.2 3.8 %collective-permute-start.8 = (f32[64,2688]{1,0:T(8,128)S(1)}, f32[64,2688]{1,0:T(8,128)S(1)}, u32[]{:S(2)}, u32[]{:S(2)}) collective-permute-start(f32[64,2688]{1,0:T(8,128)S(1)} %pad_maximum_fusion.1), channel_id=1, source_target_pairs={{0,1},{1,0},{2,3},{3,2},{4,5},{5,4},{6,7},{7,6},{8,9},{9,8},{10,11... | collective-permute-start | bytes 2064392 | tf_op jit(solution)/shard_map/ppermute | solution.py:26
  33.9 8.4 %collective-permute-start.3 = (f32[64,2688]{1,0:T(8,128)S(1)}, f32[64,2688]{1,0:T(8,128)S(1)}, u32[]{:S(2)}, u32[]{:S(2)}) collective-permute-start(f32[64,2688]{1,0:T(8,128)S(1)} %pad_maximum_fusion), channel_id=1, source_target_pairs={{0,1},{1,0},{2,3},{3,2},{4,5},{5,4},{6,7},{7,6},{8,9},{9,8},{10,11... | collective-permute-start | bytes 2064392 | tf_op jit(solution)/shard_map/ppermute | solution.py:26
  34.1 4.3 %copy-start.1 = (f32[2688,672]{0,1:T(8,128)S(1)}, f32[2688,672]{0,1:T(8,128)}, u32[]{:S(2)}) copy-start(f32[2688,672]{0,1:T(8,128)} %param.7) | copy-start | bytes 21676036
  37.1 11.0 %collective-permute-start.9 = (f32[128,672]{0,1:T(8,128)S(1)}, f32[128,672]{0,1:T(8,128)S(1)}, u32[]{:S(2)}, u32[]{:S(2)}) collective-permute-start(f32[128,672]{0,1:T(8,128)S(1)} %fusion.8), channel_id=1, source_target_pairs={{0,16},{16,0},{1,17},{17,1},{2,18},{18,2},{3,19},{19,3},{4,20},{20... | collective-permute-start | bytes 1032200 | tf_op jit(solution)/shard_map/ppermute | solution.py:26
  38.4 3.9 %copy-start.2 = (f32[672,2688]{1,0:T(8,128)S(1)}, f32[672,2688]{1,0:T(8,128)}, u32[]{:S(2)}) copy-start(f32[672,2688]{1,0:T(8,128)} %param.9) | copy-start | bytes 21676036
  41.4 14.1 %collective-permute-start.10 = (f32[128,672]{0,1:T(8,128)S(1)}, f32[128,672]{0,1:T(8,128)S(1)}, u32[]{:S(2)}, u32[]{:S(2)}) collective-permute-start(f32[128,672]{0,1:T(8,128)S(1)} %fusion.9), channel_id=1, source_target_pairs={{0,16},{16,0},{1,17},{17,1},{2,18},{18,2},{3,19},{19,3},{4,20},{20... | collective-permute-start | bytes 1032200 | tf_op jit(solution)/shard_map/ppermute | solution.py:26
  45.3 17.1 %collective-permute-start.4 = (f32[128,672]{0,1:T(8,128)S(1)}, f32[128,672]{0,1:T(8,128)S(1)}, u32[]{:S(2)}, u32[]{:S(2)}) collective-permute-start(f32[128,672]{0,1:T(8,128)S(1)} %fusion.7), channel_id=1, source_target_pairs={{0,16},{16,0},{1,17},{17,1},{2,18},{18,2},{3,19},{19,3},{4,20},{20... | collective-permute-start | bytes 1032200 | tf_op jit(solution)/shard_map/ppermute | solution.py:26
  67.8 2.2 %collective-permute-start.11 = (f32[64,2688]{1,0:T(8,128)S(1)}, f32[64,2688]{1,0:T(8,128)S(1)}, u32[]{:S(2)}, u32[]{:S(2)}) collective-permute-start(f32[64,2688]{1,0:T(8,128)S(1)} %slice.33), channel_id=1, source_target_pairs={{0,1},{1,0},{2,3},{3,2},{4,5},{5,4},{6,7},{7,6},{8,9},{9,8},{10,11... | collective-permute-start | bytes 2064392 | tf_op jit(solution)/shard_map/ppermute | solution.py:26
  70.1 10.2 %collective-permute-start.12 = (f32[32,2688]{1,0:T(8,128)S(1)}, f32[32,2688]{1,0:T(8,128)S(1)}, u32[]{:S(2)}, u32[]{:S(2)}) collective-permute-start(f32[32,2688]{1,0:T(8,128)S(1)} %slice.35), channel_id=1, source_target_pairs={{0,2},{1,3},{2,0},{3,1},{4,6},{5,7},{6,4},{7,5},{8,10},{9,11},{10,... | collective-permute-start | bytes 1032200 | tf_op jit(solution)/shard_map/ppermute | solution.py:26
  80.3 7.0 %collective-permute-start.13 = (f32[16,2688]{1,0:T(8,128)S(1)}, f32[16,2688]{1,0:T(8,128)S(1)}, u32[]{:S(2)}, u32[]{:S(2)}) collective-permute-start(f32[16,2688]{1,0:T(8,128)S(1)} %slice.37), channel_id=1, source_target_pairs={{0,4},{1,5},{2,6},{3,7},{4,0},{5,1},{6,2},{7,3},{8,12},{9,13},{10,... | collective-permute-start | bytes 516104 | tf_op jit(solution)/shard_map/ppermute | solution.py:26
  87.3 8.3 %collective-permute-start.14 = (f32[8,2688]{1,0:T(8,128)S(1)}, f32[8,2688]{1,0:T(8,128)S(1)}, u32[]{:S(2)}, u32[]{:S(2)}) collective-permute-start(f32[8,2688]{1,0:T(8,128)S(1)} %slice.39), channel_id=1, source_target_pairs={{0,8},{1,9},{2,10},{3,11},{4,12},{5,13},{6,14},{7,15},{8,0},{9,1},... | collective-permute-start | bytes 258056 | tf_op jit(solution)/shard_map/ppermute | solution.py:26
